TPU v7x, 512 devices: a whole 4x4x16 slice. The times are simulated.
512 devices in a mesh: dp: 32 (over y, x, core), fsdp: 16 (over z).
Axes of the slice: x: 4, y: 4, z: 16, core: 2. Of those that a mesh axis runs over, the one named last changes fastest.
Arguments:
- queries: bfloat16 [131072, 2048], P(('dp', 'fsdp')), may hold values from -600 to 600
- w_kv: bfloat16 [2, 2048, 896], P(None, 'fsdp'), may hold values from -0.1875 to 0.1875
- encodings: bfloat16 [196608, 896], P(('dp', 'fsdp')), may hold values from -6 to 6
- counts: int32 [512], P(('dp', 'fsdp')), may hold values from 48 to 384, as said below
- owner_rank: int32 [196608], P(('dp', 'fsdp')), may hold values from 0 to 31, as said below
- owner_span: int32 [196608], P(('dp', 'fsdp')), may hold values from 0 to 3, as said below
- grad_ctx: bfloat16 [131072, 2048], P(('dp', 'fsdp')), may hold values from -24 to 24
Outputs:
- grad_queries: bfloat16 [131072, 2048], P(('dp', 'fsdp'))
- grad_value: bfloat16 [2048, 896], P('fsdp')
Inputs may be any that keep to these rules, and one draw needn't show every extreme that they name: `counts`: each count is 384 divided by 1, 2, 4 or 8; among the devices of equal fsdp index one holds 384. `owner_rank`: among the live rows of one device at most 12 name the same owner; a device whose count is 384 names every owner exactly 12 times. `owner_span`: every span of every decoder device is named by at least one live row of a device with equal fsdp index.
All inputs are finite; a program needn't handle non-finite values.
Results may differ from a plain program's by a relative error of at most 0.023.
Values may be sent and summed in bfloat16 or wider, within the bound.
No kernel may reach another device: no remote copies, remote signals or barrier semaphores. Data moves between devices by JAX's collectives and lax.ppermute only.
A program may use at most 64 MiB of HBM per device.

v0:
```python
import jax
import jax.numpy as jnp
from jax import lax
from jax.experimental import pallas as pl
from jax.experimental.pallas import tpu as pltpu
from jax.sharding import Mesh
from jax.sharding import PartitionSpec as P

HEADS = 16
HEAD_DIM = 128
SPAN = 64
ENC = 896
TOK = 256
ROWS = 384
DP = 32
CAP = 12
PLANE = 16
HALF = HEADS // 2
GROUP = HALF // 2
EXT = ENC + 128
BIG = 2.0**100
SCALE = 1.0 / HEAD_DIM**0.5
LOG2E = 1.4426950408889634


NN = (((1,), (0,)), ((), ()))
NT = (((1,), (1,)), ((), ()))
TN = (((0,), (0,)), ((), ()))


def dot(a, b, dims):
    return lax.dot_general(a, b, dims, preferred_element_type=jnp.float32)


def pack_body(count_ref, rank_ref, span_ref, enc_ref, out_ref):
    rank = rank_ref[...]
    live = lax.broadcasted_iota(jnp.int32, (1, ROWS), 1) < count_ref[0]
    owner = lax.broadcasted_iota(jnp.int32, (DP, ROWS), 0)
    hit = ((owner == rank) & live).astype(jnp.float32)
    earlier = lax.broadcasted_iota(jnp.int32, (ROWS, ROWS), 0) < lax.broadcasted_iota(jnp.int32, (ROWS, ROWS), 1)
    before = dot(hit.astype(jnp.bfloat16), earlier.astype(jnp.float32).astype(jnp.bfloat16), NN)
    slot = jnp.sum(before * hit, axis=0, keepdims=True).astype(jnp.int32)
    target = jnp.where(live, rank * CAP + slot, -1)
    place = (lax.broadcasted_iota(jnp.int32, (ROWS, ROWS), 0) == target).astype(jnp.float32).astype(jnp.bfloat16)
    spans = (lax.broadcasted_iota(jnp.int32, (128, ROWS), 0) == span_ref[...]).astype(jnp.float32).astype(jnp.bfloat16)
    out_ref[:, :ENC] = dot(place, enc_ref[...], NN).astype(jnp.bfloat16)
    out_ref[:, ENC:] = dot(place, spans, NT).astype(jnp.bfloat16)


def pack(counts, rank, span, enc, interpret=False):
    vmem = pl.BlockSpec(memory_space=pltpu.VMEM)
    return pl.pallas_call(
        pack_body,
        out_shape=jax.ShapeDtypeStruct((ROWS, EXT), jnp.bfloat16),
        in_specs=[pl.BlockSpec(memory_space=pltpu.SMEM), vmem, vmem, vmem],
        out_specs=vmem,
        interpret=interpret,
        name="pack",
    )(counts, rank.reshape(1, ROWS), span.reshape(1, ROWS), enc)


def choose(i, options):
    result = options[-1]
    for k in range(len(options) - 2, -1, -1):
        result = jnp.where(i == k, options[k], result)
    return result


def head_of(i, place, offsets):
    even, odd = offsets
    turn = jnp.where((place[0] + place[1]) % 2 == 0, choose(i, even), choose(i, odd))
    return (place[1] + turn + HEADS) % HEADS


NEAR = ((2, -2, 4, 0), (1, -1, 3, -3))
FAR = ((-4, 6, -6, 8), (5, -5, 7, -7))


def attend_step(rows_ref, mask_ref, q_ref, g_ref, q2_ref, g2_ref, w_ref, gq_ref, gq2_ref, part_ref, dval_ref):
    step = pl.program_id(0)
    rows = rows_ref[...]
    pair = dot(rows, w_ref[...], NT).astype(jnp.bfloat16)
    token = lax.broadcasted_iota(jnp.int32, (TOK, 128), 0)
    spans = (lax.broadcasted_iota(jnp.int32, (TOK, 128), 1) == token // SPAN).astype(jnp.float32).astype(jnp.bfloat16)
    for k, (q, g, out_ref) in enumerate(((q_ref, g_ref, gq_ref), (q2_ref, g2_ref, gq2_ref))):
        at = slice(k * ROWS, (k + 1) * ROWS)
        key, value = pair[at, :HEAD_DIM], pair[at, HEAD_DIM:]
        scores = dot(jnp.concatenate([q[...], spans], 1), jnp.concatenate([key, mask_ref[at, :]], 1), NT)
        highest = jnp.max(scores, axis=1, keepdims=True)
        weights = jnp.exp2((scores - highest) * (SCALE * LOG2E))
        probs = weights * (1.0 / jnp.sum(weights, axis=1, keepdims=True))
        low = probs.astype(jnp.bfloat16)
        dprob = dot(g[...], value, NT)
        delta = jnp.sum(low.astype(jnp.float32) * dprob, axis=1, keepdims=True)
        dscore = (probs * (dprob - delta)).astype(jnp.bfloat16)
        out_ref[...] = (dot(dscore, key, NN) * SCALE).astype(jnp.bfloat16)
        turned = dot(g[...], low, TN).astype(jnp.bfloat16)
        dval_ref[pl.ds(pl.multiple_of(step * HEAD_DIM, HEAD_DIM), HEAD_DIM), at] = turned

    @pl.when(step == GROUP - 1)
    def _():
        partial = dot(dval_ref[...], rows, NN)
        for j in range(GROUP):
            block = partial[j * HEAD_DIM : (j + 1) * HEAD_DIM]
            part_ref[:, j, :, :] = block.reshape(PLANE, 8, ENC).astype(jnp.bfloat16)


def near_body(
    place_ref, own_ref, other_ref, q_ref, g_ref, q2_ref, g2_ref, w0_ref, w1_ref, w2_ref, w3_ref,
    gq_ref, gq2_ref, part_ref, rows_ref, mask_ref, w_ref, dval_ref,
):
    step = pl.program_id(0)

    @pl.when(step == 0)
    def _():
        row = lax.broadcasted_iota(jnp.int32, (ROWS, ROWS), 0)
        col = lax.broadcasted_iota(jnp.int32, (ROWS, ROWS), 1)
        second = row // (ROWS // 2)
        rest = row - second * (ROWS // 2)
        chip = rest // CAP
        owner = jnp.where(place_ref[0] == 0, second, 1 - second)
        source = chip * (2 * CAP) + owner * CAP + (rest - chip * CAP)
        select = (source == col).astype(jnp.float32).astype(jnp.bfloat16)
        lane = lax.broadcasted_iota(jnp.int32, (ROWS // 2, 128), 1)
        for k, ref in enumerate((own_ref, other_ref)):
            moved = dot(select, ref[...], NN)
            for p in range(2):
                part = moved[p * (ROWS // 2) : (p + 1) * (ROWS // 2)]
                at = pl.ds(p * ROWS + k * (ROWS // 2), ROWS // 2)
                rows_ref[at, :] = part[:, :ENC].astype(jnp.bfloat16)
                mask_ref[at, :] = jnp.where(lane < 4, (part[:, ENC:] - 1.0) * BIG, 0.0).astype(jnp.bfloat16)

    for j, ref in enumerate((w0_ref, w1_ref, w2_ref, w3_ref)):

        @pl.when(step == j)
        def _(ref=ref):
            w_ref[...] = ref[...].reshape(2 * HEAD_DIM, ENC)

    attend_step(rows_ref, mask_ref, q_ref, g_ref, q2_ref, g2_ref, w_ref, gq_ref, gq2_ref, part_ref, dval_ref)


def far_body(
    place_ref, rows_ref, mask_ref, q_ref, g_ref, q2_ref, g2_ref, wk_ref, wv_ref, a0, a1, a2,
    gq_ref, gq2_ref, part_ref, w_ref, dval_ref,
):
    w_ref[:HEAD_DIM, :] = wk_ref[...].reshape(HEAD_DIM, ENC)
    w_ref[HEAD_DIM:, :] = wv_ref[...].reshape(HEAD_DIM, ENC)
    attend_step(rows_ref, mask_ref, q_ref, g_ref, q2_ref, g2_ref, w_ref, gq_ref, gq2_ref, part_ref, dval_ref)


WIDE = jax.ShapeDtypeStruct((TOK, HEADS * HEAD_DIM), jnp.bfloat16)
PART = jax.ShapeDtypeStruct((PLANE, HALF, 8, ENC), jnp.bfloat16)


def whole(*shape):
    return pl.BlockSpec(shape, lambda i, place: (0,) * len(shape))


def head_block(offsets):
    return pl.BlockSpec((TOK, HEAD_DIM), lambda i, place: (0, head_of(i, place, offsets)))


def part_block(group):
    return pl.BlockSpec((PLANE, GROUP, 8, ENC), lambda i, place: (0, group, 0, 0))


WORK = [pltpu.VMEM((2 * HEAD_DIM, ENC), jnp.bfloat16), pltpu.VMEM((GROUP * HEAD_DIM, 2 * ROWS), jnp.bfloat16)]


def attend_near(place, own, other, tokens, weights, interpret=False):
    head = head_block(NEAR)
    return pl.pallas_call(
        near_body,
        grid_spec=pltpu.PrefetchScalarGridSpec(
            num_scalar_prefetch=1,
            grid=(GROUP,),
            in_specs=[whole(ROWS, EXT)] * 2 + [head] * 4 + [whole(2, HEAD_DIM, ENC)] * 4,
            out_specs=[head, head, part_block(0), whole(2 * ROWS, ENC), whole(2 * ROWS, 128)],
            scratch_shapes=WORK,
        ),
        out_shape=[
            WIDE,
            WIDE,
            PART,
            jax.ShapeDtypeStruct((2 * ROWS, ENC), jnp.bfloat16),
            jax.ShapeDtypeStruct((2 * ROWS, 128), jnp.bfloat16),
        ],
        interpret=interpret,
        name="near",
    )(place, own, other, *tokens, *weights)


def attend_far(place, rows, mask, tokens, weights, gq, gq2, part, interpret=False):
    head = head_block(FAR)
    kv = lambda pick: pl.BlockSpec((PLANE, 1, 1, 8, ENC), lambda i, place: (0, pick(place[0]), i, 0, 0))
    kept = pl.BlockSpec(memory_space=pl.ANY)
    return pl.pallas_call(
        far_body,
        grid_spec=pltpu.PrefetchScalarGridSpec(
            num_scalar_prefetch=1,
            grid=(GROUP,),
            in_specs=[whole(2 * ROWS, ENC), whole(2 * ROWS, 128)]
            + [head] * 4
            + [kv(lambda c: c), kv(lambda c: 1 - c)]
            + [kept] * 3,
            out_specs=[head, head, part_block(1)],
            scratch_shapes=WORK,
        ),
        out_shape=[WIDE, WIDE, PART],
        input_output_aliases={9: 0, 10: 1, 11: 2},
        interpret=interpret,
        name="far",
    )(place, rows, mask, *tokens, weights, weights, gq, gq2, part)


def deal_body(place_ref, mine_ref, theirs_ref, kept_ref, given_ref):
    kept_ref[...] = mine_ref[...]
    given_ref[...] = theirs_ref[...]


def deal(place, heads, interpret=False):
    row = lambda index: pl.BlockSpec((1, 8, ENC), index)
    out = row(lambda i, place: (i, 0, 0))
    shape = jax.ShapeDtypeStruct((GROUP, 8, ENC), jnp.bfloat16)
    return pl.pallas_call(
        deal_body,
        grid_spec=pltpu.PrefetchScalarGridSpec(
            num_scalar_prefetch=1,
            grid=(GROUP,),
            in_specs=[
                row(lambda i, place: (head_of(i, place, FAR), 0, 0)),
                row(lambda i, place: (head_of(i, place, FAR[::-1]), 0, 0)),
            ],
            out_specs=[out, out],
        ),
        out_shape=[shape, shape],
        interpret=interpret,
        name="deal",
    )(place, heads, heads)


def gather_body(place_ref, part_ref, out_ref):
    out_ref[...] = jnp.sum(part_ref[...].astype(jnp.float32), axis=0).astype(jnp.bfloat16)


def gather(place, part, interpret=False):
    both = tuple(n + f for n, f in zip(NEAR, FAR))
    return pl.pallas_call(
        gather_body,
        grid_spec=pltpu.PrefetchScalarGridSpec(
            num_scalar_prefetch=1,
            grid=(HALF,),
            in_specs=[pl.BlockSpec((PLANE, 1, 8, ENC), lambda i, place: (0, i, 0, 0))],
            out_specs=pl.BlockSpec((1, 8, ENC), lambda i, place: (head_of(i, place, both), 0, 0)),
        ),
        out_shape=jax.ShapeDtypeStruct((HEADS, 8, ENC), jnp.bfloat16),
        interpret=interpret,
        name="gather",
    )(place, part)


def swap(array):
    return lax.ppermute(array, "c", [(0, 1), (1, 0)])


def exchange(array, axis):
    return lax.all_to_all(array, axis, split_axis=0, concat_axis=0, tiled=True)


def spread(array, axis, count):
    return exchange(jnp.broadcast_to(array[None], (count,) + array.shape), axis)


def total(array):
    return array.astype(jnp.float32).sum(0)


def fetch(array, even, odd):
    pairs = []
    for c in range(2):
        for z in range(HEADS):
            turn = odd if (c + z) % 2 else even
            core = 1 - c if (turn % 2 == 0) == (even != 0) else c
            pairs.append((core * HEADS + (z + turn) % HEADS, c * HEADS + z))
    assert len({a for a, _ in pairs}) == len(pairs)
    return lax.ppermute(array, ("c", "z"), pairs)


def local(queries, w_kv, encodings, counts, owner_rank, owner_span, grad_ctx):
    c = lax.axis_index("c")
    z = lax.axis_index("z")
    place = jnp.stack([c, z]).astype(jnp.int32)
    plane = lax.axis_index("y") * 4 + lax.axis_index("x")
    piece = lax.dynamic_slice(w_kv, (c, plane * 8, 0), (1, 8, ENC))[0]
    heads = spread(piece, "z", HEADS)
    kept, given = deal(place, heads)
    mine = jnp.stack([kept, swap(given)])
    near = [fetch(w_kv, even, odd) for even, odd in zip(*NEAR)]

    packed = pack(counts, owner_rank, owner_span, encodings)
    arrived = exchange(packed.reshape(PLANE, 2 * CAP, EXT), ("y", "x")).reshape(ROWS, EXT)
    other = swap(arrived)
    weights = spread(mine, ("y", "x"), PLANE)
    tokens = (queries, grad_ctx, swap(queries), swap(grad_ctx))

    gq, gq2, part, rows, mask = attend_near(place, arrived, other, tokens, near)
    gq, gq2, part = attend_far(place, rows, mask, tokens, weights, gq, gq2, part)

    sums = gather(place, exchange(part, ("y", "x")))
    final = (total(exchange(sums, "z")) / DP).astype(jnp.bfloat16)
    block = spread(final, ("y", "x"), PLANE).reshape(HEAD_DIM, ENC)
    grad_value = jnp.where(z % 2 == c, block, swap(block))
    own_head = (lax.broadcasted_iota(jnp.int32, gq.shape, 1) // HEAD_DIM) % 2 == c
    return jnp.where(own_head, gq, swap(gq2)), grad_value


def solution(mesh):
    fine = Mesh(mesh.devices.reshape(4, 4, 2, HEADS), ("y", "x", "c", "z"))
    every = ("y", "x", "c", "z")
    in_specs = (
        P(every, None),
        P(None, "z", None),
        P(every, None),
        P(every),
        P(every),
        P(every),
        P(every, None),
    )
    out_specs = (P(every, None), P("z", None))
    return jax.shard_map(local, mesh=fine, in_specs=in_specs, out_specs=out_specs, check_vma=False)
```

profile of v0, /device:TPU:1, one launch (start us, length us, event | category | flops | bytes accessed | tf_op | source)
XLA Modules:
  0.0 238.1 jit_solution(1673737813805120739)
XLA Ops:
  2.1 15.7 %all-to-all-start.1 = ((bf16[16,8,896]{2,1,0:T(8,128)(2,1)}), bf16[16,8,896]{2,1,0:T(8,128)(2,1)S(1)}, u32[]{:S(2)}, u32[]{:S(2)}) async-start(bf16[16,8,896]{2,1,0:T(8,128)(2,1)} %broadcast_in_dim.9), calls=%async_computation.1 | async-start | bytes 458752 | tf_op jit(solution)/shard_map/all_to_all | solution.py:267
  20.9 2.8 %pack.1 = bf16[384,1024]{1,0:T(8,128)(2,1)} custom-call(s32[1]{0:T(128)S(6)} %copy.15.count_ref, s32[1,384]{1,0:T(1,128)} %reshape.24.rank_ref, s32[1,384]{1,0:T(1,128)} %reshape.25.span_ref, bf16[384,896]{1,0:T(8,128)(2,1)} %enc_ref.1), custom_call_target="tpu_custom_call" | custom-call | tf_op jit(solution)/shard_map/pack/pallas_call | solution.py:52
  23.7 6.8 %all-to-all-done.1.mine_ref.theirs_ref = bf16[16,8,896]{2,1,0:T(8,128)(2,1)S(1)} async-done(((bf16[16,8,896]{2,1,0:T(8,128)(2,1)}), bf16[16,8,896]{2,1,0:T(8,128)(2,1)S(1)}, u32[]{:S(2)}, u32[]{:S(2)}) %all-to-all-start.1) | async-done | bytes 229408 | tf_op jit(solution)/shard_map/all_to_all | solution.py:267
  30.5 6.8 %all-to-all-start = ((bf16[16,24,1024]{2,1,0:T(8,128)(2,1)}), bf16[16,24,1024]{2,1,0:T(8,128)(2,1)S(1)}, u32[]{:S(2)}, u32[]{:S(2)}) async-start(bf16[16,24,1024]{2,1,0:T(8,128)(2,1)} %bitcast.12), calls=%async_computation | async-start | bytes 1572864 | tf_op jit(solution)/shard_map/all_to_all | solution.py:267
  37.8 3.4 %deal.1 = (bf16[4,8,896]{2,1,0:T(8,128)(2,1)}, bf16[4,8,896]{2,1,0:T(8,128)(2,1)}) custom-call(s32[2]{0:T(128)} %pad_add_fusion.place_ref, bf16[16,8,896]{2,1,0:T(8,128)(2,1)} %copy-done.6, bf16[16,8,896]{2,1,0:T(8,128)(2,1)} %copy-done.6), custom_call_target="tpu_custom_call" | custom-call | tf_op jit(solution)/shard_map/deal/pallas_call | solution.py:225
  41.2 7.6 %collective-permute-start.7 = (bf16[4,8,896]{2,1,0:T(8,128)(2,1)}, bf16[4,8,896]{2,1,0:T(8,128)(2,1)S(1)}, u32[]{:S(2)}, u32[]{:S(2)}) collective-permute-start(bf16[4,8,896]{2,1,0:T(8,128)(2,1)} %get-tuple-element.15), channel_id=1, source_target_pairs={{0,16},{16,0},{1,17},{17,1},{2,18},{18,2},{3,19},{19,3},{4,20},{20... | collective-permute-start | bytes 172040 | tf_op jit(solution)/shard_map/ppermute | solution.py:263
  52.3 7.1 %all-to-all-start.2 = ((bf16[16,2,4,8,896]{4,3,2,1,0:T(8,128)(2,1)}), bf16[16,2,4,8,896]{4,3,2,1,0:T(8,128)(2,1)S(1)}, u32[]{:S(2)}, u32[]{:S(2)}) async-start(bf16[16,2,4,8,896]{4,3,2,1,0:T(8,128)(2,1)} %broadcast_in_dim.10), calls=%async_computation.2 | async-start | bytes 3670016 | tf_op jit(solution)/shard_map/all_to_all | solution.py:267
  59.4 2.5 %collective-permute-start.1 = (bf16[256,2048]{1,0:T(8,128)(2,1)S(1)}, bf16[256,2048]{1,0:T(8,128)(2,1)S(1)}, u32[]{:S(2)}, u32[]{:S(2)}) collective-permute-start(bf16[256,2048]{1,0:T(8,128)(2,1)S(1)} %copy-done.2), channel_id=1, source_target_pairs={{0,16},{16,0},{1,17},{17,1},{2,18},{18,2},{3,19},{19,3},{4,20},{20... | collective-permute-start | bytes 3145736 | tf_op jit(solution)/shard_map/ppermute | solution.py:263
  63.9 6.2 %collective-permute-start.3 = (bf16[2,128,896]{2,1,0:T(8,128)(2,1)}, bf16[2,128,896]{2,1,0:T(8,128)(2,1)S(1)}, u32[]{:S(2)}, u32[]{:S(2)}) collective-permute-start(bf16[2,128,896]{2,1,0:T(8,128)(2,1)} %param.8), channel_id=1, source_target_pairs={{18,0},{2,1},{20,2},{4,3},{22,4},{6,5},{24,6},{8,7},{26,8},{10,9},... | collective-permute-start | bytes 1376264 | tf_op jit(solution)/shard_map/ppermute | solution.py:286
  70.1 3.1 %collective-permute-start.4 = (bf16[2,128,896]{2,1,0:T(8,128)(2,1)}, bf16[2,128,896]{2,1,0:T(8,128)(2,1)S(1)}, u32[]{:S(2)}, u32[]{:S(2)}) collective-permute-start(bf16[2,128,896]{2,1,0:T(8,128)(2,1)} %param.8), channel_id=1, source_target_pairs={{30,0},{0,1},{16,2},{2,3},{18,4},{4,5},{20,6},{6,7},{22,8},{8,9},{... | collective-permute-start | bytes 1376264 | tf_op jit(solution)/shard_map/ppermute | solution.py:286
  75.0 10.5 %collective-permute-done.3.w0_ref = bf16[2,128,896]{2,1,0:T(8,128)(2,1)S(1)} collective-permute-done((bf16[2,128,896]{2,1,0:T(8,128)(2,1)}, bf16[2,128,896]{2,1,0:T(8,128)(2,1)S(1)}, u32[]{:S(2)}, u32[]{:S(2)}) %collective-permute-start.3) | collective-permute-done | bytes 458784 | tf_op jit(solution)/shard_map/ppermute | solution.py:286
  87.6 2.2 collective-permute-done.4.w1_ref
  89.7 4.3 %collective-permute-start.6 = (bf16[2,128,896]{2,1,0:T(8,128)(2,1)}, bf16[2,128,896]{2,1,0:T(8,128)(2,1)S(1)}, u32[]{:S(2)}, u32[]{:S(2)}) collective-permute-start(bf16[2,128,896]{2,1,0:T(8,128)(2,1)} %param.8), channel_id=1, source_target_pairs={{0,0},{30,1},{2,2},{16,3},{4,4},{18,5},{6,6},{20,7},{8,8},{22,9},{... | collective-permute-start | bytes 1376264 | tf_op jit(solution)/shard_map/ppermute | solution.py:286
  94.0 31.8 %collective-permute-done.5.w2_ref = bf16[2,128,896]{2,1,0:T(8,128)(2,1)S(1)} collective-permute-done((bf16[2,128,896]{2,1,0:T(8,128)(2,1)}, bf16[2,128,896]{2,1,0:T(8,128)(2,1)S(1)}, u32[]{:S(2)}, u32[]{:S(2)}) %collective-permute-start.5) | collective-permute-done | bytes 458784 | tf_op jit(solution)/shard_map/ppermute | solution.py:286
  128.1 16.3 %near.1 = (bf16[256,2048]{1,0:T(8,128)(2,1)}, bf16[256,2048]{1,0:T(8,128)(2,1)}, bf16[16,8,8,896]{3,2,1,0:T(8,128)(2,1)}, bf16[768,896]{1,0:T(8,128)(2,1)}, bf16[768,128]{1,0:T(8,128)(2,1)}) custom-call(s32[2]{0:T(128)} %pad_add_fusion.place_ref, bf16[384,1024]{1,0:T(8,128)(2,1)} %bitcast.11, bf16[384,1024]{1,0:T(8,128)(2,1)} %collective-permute-done.other_ref, ...), custom_call_target="tpu_custom_call" | custom-call | tf_op jit(solution)/shard_map/near/pallas_call | solution.py:172
  145.7 14.3 %far.1 = (bf16[256,2048]{1,0:T(8,128)(2,1)}, bf16[256,2048]{1,0:T(8,128)(2,1)}, bf16[16,8,8,896]{3,2,1,0:T(8,128)(2,1)}) custom-call(s32[2]{0:T(128)} %pad_add_fusion.place_ref, bf16[768,896]{1,0:T(8,128)(2,1)} %get-tuple-element.12.rows_ref, ...), custom_call_target="tpu_custom_call", output_to_operand_aliasing={{0}: (9, {}), {1}: (10, {}), {2}: (11, {})} | custom-call | tf_op jit(solution)/shard_map/far/pallas_call | solution.py:197
  160.0 32.4 %all_to_all.30.part_ref = bf16[16,8,8,896]{3,2,1,0:T(8,128)(2,1)} all-to-all(bf16[16,8,8,896]{3,2,1,0:T(8,128)(2,1)} %get-tuple-element.21), channel_id=1, replica_groups=mesh['y'=4,'x'=4,'c'=2,'z'=16] {'y','x'}, dimensions={0} | all-to-all | bytes 3670016 | tf_op jit(solution)/shard_map/all_to_all | solution.py:267
  192.4 6.1 %gather.1 = bf16[16,8,896]{2,1,0:T(8,128)(2,1)} custom-call(s32[2]{0:T(128)} %pad_add_fusion.place_ref, bf16[16,8,8,896]{3,2,1,0:T(8,128)(2,1)} %all_to_all.30.part_ref), custom_call_target="tpu_custom_call" | custom-call | tf_op jit(solution)/shard_map/gather/pallas_call | solution.py:248
  198.5 3.5 %all-to-all-start.4 = ((bf16[16,8,896]{2,1,0:T(8,128)(2,1)}), bf16[16,8,896]{2,1,0:T(8,128)(2,1)S(1)}, u32[]{:S(2)}, u32[]{:S(2)}) async-start(bf16[16,8,896]{2,1,0:T(8,128)(2,1)} %gather.1), calls=%async_computation.4 | async-start | bytes 458752 | tf_op jit(solution)/shard_map/all_to_all | solution.py:267
  202.0 5.4 %collective-permute-start.8 = (bf16[256,2048]{1,0:T(8,128)(2,1)S(1)}, bf16[256,2048]{1,0:T(8,128)(2,1)S(1)}, u32[]{:S(2)}, u32[]{:S(2)}) collective-permute-start(bf16[256,2048]{1,0:T(8,128)(2,1)S(1)} %copy-done.7), channel_id=1, source_target_pairs={{0,16},{16,0},{1,17},{17,1},{2,18},{18,2},{3,19},{19,3},{4,20},{20... | collective-permute-start | bytes 3145736 | tf_op jit(solution)/shard_map/ppermute | solution.py:263
  207.5 7.0 %all-to-all-done.4 = bf16[16,8,896]{2,1,0:T(8,128)(2,1)S(1)} async-done(((bf16[16,8,896]{2,1,0:T(8,128)(2,1)}), bf16[16,8,896]{2,1,0:T(8,128)(2,1)S(1)}, u32[]{:S(2)}, u32[]{:S(2)}) %all-to-all-start.4) | async-done | bytes 229408 | tf_op jit(solution)/shard_map/all_to_all | solution.py:267
  215.2 3.5 %all-to-all-start.5 = ((bf16[16,8,896]{2,1,0:T(8,128)(2,1)}), bf16[16,8,896]{2,1,0:T(8,128)(2,1)S(1)}, u32[]{:S(2)}, u32[]{:S(2)}) async-start(bf16[16,8,896]{2,1,0:T(8,128)(2,1)} %broadcast_in_dim.22), calls=%async_computation.5 | async-start | bytes 458752 | tf_op jit(solution)/shard_map/all_to_all | solution.py:267
  218.8 7.3 %all-to-all-done.5 = bf16[16,8,896]{2,1,0:T(8,128)(2,1)S(1)} async-done(((bf16[16,8,896]{2,1,0:T(8,128)(2,1)}), bf16[16,8,896]{2,1,0:T(8,128)(2,1)S(1)}, u32[]{:S(2)}, u32[]{:S(2)}) %all-to-all-start.5) | async-done | bytes 229408 | tf_op jit(solution)/shard_map/all_to_all | solution.py:267
  226.1 9.7 %collective-permute-start.9 = (bf16[128,896]{1,0:T(8,128)(2,1)S(1)}, bf16[128,896]{1,0:T(8,128)(2,1)S(1)}, u32[]{:S(2)}, u32[]{:S(2)}) collective-permute-start(bf16[128,896]{1,0:T(8,128)(2,1)S(1)} %bitcast.13), channel_id=1, source_target_pairs={{0,16},{16,0},{1,17},{17,1},{2,18},{18,2},{3,19},{19,3},{4,20},{20... | collective-permute-start | bytes 688136 | tf_op jit(solution)/shard_map/ppermute | solution.py:263
  (50 shorter events, 20.3 us)
Async XLA Ops:
  2.1 28.4 %all-to-all-start.1 = ((bf16[16,8,896]{2,1,0:T(8,128)(2,1)}), bf16[16,8,896]{2,1,0:T(8,128)(2,1)S(1)}, u32[]{:S(2)}, u32[]{:S(2)}) async-start(bf16[16,8,896]{2,1,0:T(8,128)(2,1)} %broadcast_in_dim.9), calls=%async_computation.1 | async-start | bytes 458752 | tf_op jit(solution)/shard_map/all_to_all | solution.py:267
  30.5 7.4 %copy-start.6 = (bf16[16,8,896]{2,1,0:T(8,128)(2,1)}, bf16[16,8,896]{2,1,0:T(8,128)(2,1)S(1)}, u32[]{:S(2)}) copy-start(bf16[16,8,896]{2,1,0:T(8,128)(2,1)S(1)} %all-to-all-done.1.mine_ref.theirs_ref) | copy-start | bytes 688132
  30.5 20.3 %all-to-all-start = ((bf16[16,24,1024]{2,1,0:T(8,128)(2,1)}), bf16[16,24,1024]{2,1,0:T(8,128)(2,1)S(1)}, u32[]{:S(2)}, u32[]{:S(2)}) async-start(bf16[16,24,1024]{2,1,0:T(8,128)(2,1)} %bitcast.12), calls=%async_computation | async-start | bytes 1572864 | tf_op jit(solution)/shard_map/all_to_all | solution.py:267
  41.2 8.7 %collective-permute-start.7 = (bf16[4,8,896]{2,1,0:T(8,128)(2,1)}, bf16[4,8,896]{2,1,0:T(8,128)(2,1)S(1)}, u32[]{:S(2)}, u32[]{:S(2)}) collective-permute-start(bf16[4,8,896]{2,1,0:T(8,128)(2,1)} %get-tuple-element.15), channel_id=1, source_target_pairs={{0,16},{16,0},{1,17},{17,1},{2,18},{18,2},{3,19},{19,3},{4,20},{20... | collective-permute-start | bytes 172040 | tf_op jit(solution)/shard_map/ppermute | solution.py:263
  50.8 1.5 copy-start.5
  52.3 7.1 %copy-start.2 = (bf16[256,2048]{1,0:T(8,128)(2,1)S(1)}, bf16[256,2048]{1,0:T(8,128)(2,1)}, u32[]{:S(2)}) copy-start(bf16[256,2048]{1,0:T(8,128)(2,1)} %q_ref.3) | copy-start | bytes 3145732
  52.3 92.1 %all-to-all-start.2 = ((bf16[16,2,4,8,896]{4,3,2,1,0:T(8,128)(2,1)}), bf16[16,2,4,8,896]{4,3,2,1,0:T(8,128)(2,1)S(1)}, u32[]{:S(2)}, u32[]{:S(2)}) async-start(bf16[16,2,4,8,896]{4,3,2,1,0:T(8,128)(2,1)} %broadcast_in_dim.10), calls=%async_computation.2 | async-start | bytes 3670016 | tf_op jit(solution)/shard_map/all_to_all | solution.py:267
  59.4 66.5 %collective-permute-start.1 = (bf16[256,2048]{1,0:T(8,128)(2,1)S(1)}, bf16[256,2048]{1,0:T(8,128)(2,1)S(1)}, u32[]{:S(2)}, u32[]{:S(2)}) collective-permute-start(bf16[256,2048]{1,0:T(8,128)(2,1)S(1)} %copy-done.2), channel_id=1, source_target_pairs={{0,16},{16,0},{1,17},{17,1},{2,18},{18,2},{3,19},{19,3},{4,20},{20... | collective-permute-start | bytes 3145736 | tf_op jit(solution)/shard_map/ppermute | solution.py:263
  61.9 64.9 %collective-permute-start.2 = (bf16[256,2048]{1,0:T(8,128)(2,1)}, bf16[256,2048]{1,0:T(8,128)(2,1)S(1)}, u32[]{:S(2)}, u32[]{:S(2)}) collective-permute-start(bf16[256,2048]{1,0:T(8,128)(2,1)} %g_ref.3), channel_id=1, source_target_pairs={{0,16},{16,0},{1,17},{17,1},{2,18},{18,2},{3,19},{19,3},{4,20},{20... | collective-permute-start | bytes 3145736 | tf_op jit(solution)/shard_map/ppermute | solution.py:263
  63.9 21.7 %collective-permute-start.3 = (bf16[2,128,896]{2,1,0:T(8,128)(2,1)}, bf16[2,128,896]{2,1,0:T(8,128)(2,1)S(1)}, u32[]{:S(2)}, u32[]{:S(2)}) collective-permute-start(bf16[2,128,896]{2,1,0:T(8,128)(2,1)} %param.8), channel_id=1, source_target_pairs={{18,0},{2,1},{20,2},{4,3},{22,4},{6,5},{24,6},{8,7},{26,8},{10,9},... | collective-permute-start | bytes 1376264 | tf_op jit(solution)/shard_map/ppermute | solution.py:286
  70.1 19.7 %collective-permute-start.4 = (bf16[2,128,896]{2,1,0:T(8,128)(2,1)}, bf16[2,128,896]{2,1,0:T(8,128)(2,1)S(1)}, u32[]{:S(2)}, u32[]{:S(2)}) collective-permute-start(bf16[2,128,896]{2,1,0:T(8,128)(2,1)} %param.8), channel_id=1, source_target_pairs={{30,0},{0,1},{16,2},{2,3},{18,4},{4,5},{20,6},{6,7},{22,8},{8,9},{... | collective-permute-start | bytes 1376264 | tf_op jit(solution)/shard_map/ppermute | solution.py:286
  73.1 55.0 %collective-permute-start = (bf16[384,1024]{1,0:T(8,128)(2,1)}, bf16[384,1024]{1,0:T(8,128)(2,1)}, u32[]{:S(2)}, u32[]{:S(2)}) collective-permute-start(bf16[384,1024]{1,0:T(8,128)(2,1)} %bitcast.10), channel_id=1, source_target_pairs={{0,16},{16,0},{1,17},{17,1},{2,18},{18,2},{3,19},{19,3},{4,20},{20... | collective-permute-start | bytes 2359304 | tf_op jit(solution)/shard_map/ppermute | solution.py:263
  85.5 42.5 %copy-start.8 = (bf16[2,128,896]{2,1,0:T(8,128)(2,1)}, bf16[2,128,896]{2,1,0:T(8,128)(2,1)S(1)}, u32[]{:S(2)}) copy-start(bf16[2,128,896]{2,1,0:T(8,128)(2,1)S(1)} %collective-permute-done.3.w0_ref) | copy-start | bytes 1376260
  85.5 40.3 %collective-permute-start.5 = (bf16[2,128,896]{2,1,0:T(8,128)(2,1)}, bf16[2,128,896]{2,1,0:T(8,128)(2,1)S(1)}, u32[]{:S(2)}, u32[]{:S(2)}) collective-permute-start(bf16[2,128,896]{2,1,0:T(8,128)(2,1)} %param.8), channel_id=1, source_target_pairs={{20,0},{4,1},{22,2},{6,3},{24,4},{8,5},{26,6},{10,7},{28,8},{12,9}... | collective-permute-start | bytes 1376264 | tf_op jit(solution)/shard_map/ppermute | solution.py:286
  89.7 37.1 %copy-start.9 = (bf16[2,128,896]{2,1,0:T(8,128)(2,1)}, bf16[2,128,896]{2,1,0:T(8,128)(2,1)S(1)}, u32[]{:S(2)}) copy-start(bf16[2,128,896]{2,1,0:T(8,128)(2,1)S(1)} %collective-permute-done.4.w1_ref) | copy-start | bytes 1376260
  89.7 36.1 %collective-permute-start.6 = (bf16[2,128,896]{2,1,0:T(8,128)(2,1)}, bf16[2,128,896]{2,1,0:T(8,128)(2,1)S(1)}, u32[]{:S(2)}, u32[]{:S(2)}) collective-permute-start(bf16[2,128,896]{2,1,0:T(8,128)(2,1)} %param.8), channel_id=1, source_target_pairs={{0,0},{30,1},{2,2},{16,3},{4,4},{18,5},{6,6},{20,7},{8,8},{22,9},{... | collective-permute-start | bytes 1376264 | tf_op jit(solution)/shard_map/ppermute | solution.py:286
  125.8 1.2 copy-start.11
  144.4 1.3 copy-start
  192.4 9.6 %copy-start.7 = (bf16[256,2048]{1,0:T(8,128)(2,1)S(1)}, bf16[256,2048]{1,0:T(8,128)(2,1)}, u32[]{:S(2)}) copy-start(bf16[256,2048]{1,0:T(8,128)(2,1)} %get-tuple-element.20) | copy-start | bytes 3145732
  192.4 43.4 %copy-start.1 = (bf16[256,2048]{1,0:T(8,128)(2,1)S(1)}, bf16[256,2048]{1,0:T(8,128)(2,1)}, u32[]{:S(2)}) copy-start(bf16[256,2048]{1,0:T(8,128)(2,1)} %get-tuple-element.19) | copy-start | bytes 3145732
  198.5 16.0 %all-to-all-start.4 = ((bf16[16,8,896]{2,1,0:T(8,128)(2,1)}), bf16[16,8,896]{2,1,0:T(8,128)(2,1)S(1)}, u32[]{:S(2)}, u32[]{:S(2)}) async-start(bf16[16,8,896]{2,1,0:T(8,128)(2,1)} %gather.1), calls=%async_computation.4 | async-start | bytes 458752 | tf_op jit(solution)/shard_map/all_to_all | solution.py:267
  202.0 33.8 %collective-permute-start.8 = (bf16[256,2048]{1,0:T(8,128)(2,1)S(1)}, bf16[256,2048]{1,0:T(8,128)(2,1)S(1)}, u32[]{:S(2)}, u32[]{:S(2)}) collective-permute-start(bf16[256,2048]{1,0:T(8,128)(2,1)S(1)} %copy-done.7), channel_id=1, source_target_pairs={{0,16},{16,0},{1,17},{17,1},{2,18},{18,2},{3,19},{19,3},{4,20},{20... | collective-permute-start | bytes 3145736 | tf_op jit(solution)/shard_map/ppermute | solution.py:263
  215.2 10.9 %all-to-all-start.5 = ((bf16[16,8,896]{2,1,0:T(8,128)(2,1)}), bf16[16,8,896]{2,1,0:T(8,128)(2,1)S(1)}, u32[]{:S(2)}, u32[]{:S(2)}) async-start(bf16[16,8,896]{2,1,0:T(8,128)(2,1)} %broadcast_in_dim.22), calls=%async_computation.5 | async-start | bytes 458752 | tf_op jit(solution)/shard_map/all_to_all | solution.py:267
  226.1 11.3 %collective-permute-start.9 = (bf16[128,896]{1,0:T(8,128)(2,1)S(1)}, bf16[128,896]{1,0:T(8,128)(2,1)S(1)}, u32[]{:S(2)}, u32[]{:S(2)}) collective-permute-start(bf16[128,896]{1,0:T(8,128)(2,1)S(1)} %bitcast.13), channel_id=1, source_target_pairs={{0,16},{16,0},{1,17},{17,1},{2,18},{18,2},{3,19},{19,3},{4,20},{20... | collective-permute-start | bytes 688136 | tf_op jit(solution)/shard_map/ppermute | solution.py:263
  (3 other events, 3.1 us)
where the time goes:
time: 240 us; the launch traced here: 238 us
  starting transfers between devices  81.3 us (34%)
  waiting for transfers between devices  66.6 us (28%)
  Pallas kernels  42.8 us (18%)
  blocking collectives  32.4 us (14%)
  local copies, waits for them, and re-layouts  9.61 us (4%)
  other arithmetic  3.75 us (2%)
    ppermute x4, waiting for transfers between devices, fetch(): return lax.ppermute(array, ('c', 'z'), pairs)  44.5 us
    all_to_all x5, starting transfers between devices, exchange(): return lax.all_to_all(array, axis, split_axis=0, concat_axis=0, tiled=True)  36.6 us
    all_to_all x1, blocking collectives, exchange(): return lax.all_to_all(array, axis, split_axis=0, concat_axis=0, tiled=True)  32.4 us
    ppermute x6, starting transfers between devices, swap(): return lax.ppermute(array, 'c', [(0, 1), (1, 0)])  29.1 us
    all_to_all x5, waiting for transfers between devices, exchange(): return lax.all_to_all(array, axis, split_axis=0, concat_axis=0, tiled=True)  21.1 us
    pallas_call x1, Pallas kernels, attend_near(): pl.pallas_call(near_body, grid_spec=pltpu.PrefetchScalarGridSpec(num_scal...  16.3 us
    ppermute x4, starting transfers between devices, fetch(): return lax.ppermute(array, ('c', 'z'), pairs)  15.5 us
    pallas_call x1, Pallas kernels, attend_far(): pl.pallas_call(far_body, grid_spec=pltpu.PrefetchScalarGridSpec(num_scala...  14.3 us
  transfers between devices with their start and end apart: 15, of which 7 were waited for; matrix products, arithmetic and copies ran while one was open for 3% of the time, Pallas kernels for 9%

commit v1 on v0

--- a/solution.py
+++ b/solution.py
@@ -15,8 +15,6 @@
 DP = 32
 CAP = 12
 PLANE = 16
-HALF = HEADS // 2
-GROUP = HALF // 2
 EXT = ENC + 128
 BIG = 2.0**100
 SCALE = 1.0 / HEAD_DIM**0.5
@@ -59,25 +57,28 @@
     )(counts, rank.reshape(1, ROWS), span.reshape(1, ROWS), enc)
 
 
+NEAR = ((2, -2, 0), (1, -1, 3), (1, -1, -3))
+FAR = ((4, -4, 6, -6, 8), (-3, 5, -5, 7, -7), (3, 5, -5, 7, -7))
+
+
 def choose(i, options):
+    if isinstance(i, int):
+        return options[i]
     result = options[-1]
     for k in range(len(options) - 2, -1, -1):
         result = jnp.where(i == k, options[k], result)
     return result
 
 
-def head_of(i, place, offsets):
-    even, odd = offsets
-    turn = jnp.where((place[0] + place[1]) % 2 == 0, choose(i, even), choose(i, odd))
-    return (place[1] + turn + HEADS) % HEADS
-
-
-NEAR = ((2, -2, 4, 0), (1, -1, 3, -3))
-FAR = ((-4, 6, -6, 8), (5, -5, 7, -7))
+def head_of(i, c, z, offsets):
+    even, first, second = (choose(i, row) for row in offsets)
+    turn = jnp.where((c + z) % 2 == 0, even, jnp.where(c == 0, first, second))
+    return (z + turn + HEADS) % HEADS
 
 
 def attend_step(rows_ref, mask_ref, q_ref, g_ref, q2_ref, g2_ref, w_ref, gq_ref, gq2_ref, part_ref, dval_ref):
     step = pl.program_id(0)
+    group = part_ref.shape[1]
     rows = rows_ref[...]
     pair = dot(rows, w_ref[...], NT).astype(jnp.bfloat16)
     token = lax.broadcasted_iota(jnp.int32, (TOK, 128), 0)
@@ -97,16 +98,16 @@
         turned = dot(g[...], low, TN).astype(jnp.bfloat16)
         dval_ref[pl.ds(pl.multiple_of(step * HEAD_DIM, HEAD_DIM), HEAD_DIM), at] = turned
 
-    @pl.when(step == GROUP - 1)
+    @pl.when(step == group - 1)
     def _():
         partial = dot(dval_ref[...], rows, NN)
-        for j in range(GROUP):
+        for j in range(group):
             block = partial[j * HEAD_DIM : (j + 1) * HEAD_DIM]
             part_ref[:, j, :, :] = block.reshape(PLANE, 8, ENC).astype(jnp.bfloat16)
 
 
 def near_body(
-    place_ref, own_ref, other_ref, q_ref, g_ref, q2_ref, g2_ref, w0_ref, w1_ref, w2_ref, w3_ref,
+    place_ref, own_ref, other_ref, q_ref, g_ref, q2_ref, g2_ref, w0_ref, w1_ref, w2_ref,
     gq_ref, gq2_ref, part_ref, rows_ref, mask_ref, w_ref, dval_ref,
 ):
     step = pl.program_id(0)
@@ -130,7 +131,7 @@
                 rows_ref[at, :] = part[:, :ENC].astype(jnp.bfloat16)
                 mask_ref[at, :] = jnp.where(lane < 4, (part[:, ENC:] - 1.0) * BIG, 0.0).astype(jnp.bfloat16)
 
-    for j, ref in enumerate((w0_ref, w1_ref, w2_ref, w3_ref)):
+    for j, ref in enumerate((w0_ref, w1_ref, w2_ref)):
 
         @pl.when(step == j)
         def _(ref=ref):
@@ -140,7 +141,7 @@
 
 
 def far_body(
-    place_ref, rows_ref, mask_ref, q_ref, g_ref, q2_ref, g2_ref, wk_ref, wv_ref, a0, a1, a2,
+    place_ref, rows_ref, mask_ref, q_ref, g_ref, q2_ref, g2_ref, wk_ref, wv_ref, a0, a1,
     gq_ref, gq2_ref, part_ref, w_ref, dval_ref,
 ):
     w_ref[:HEAD_DIM, :] = wk_ref[...].reshape(HEAD_DIM, ENC)
@@ -149,7 +150,6 @@
 
 
 WIDE = jax.ShapeDtypeStruct((TOK, HEADS * HEAD_DIM), jnp.bfloat16)
-PART = jax.ShapeDtypeStruct((PLANE, HALF, 8, ENC), jnp.bfloat16)
 
 
 def whole(*shape):
@@ -157,31 +157,33 @@
 
 
 def head_block(offsets):
-    return pl.BlockSpec((TOK, HEAD_DIM), lambda i, place: (0, head_of(i, place, offsets)))
-
-
-def part_block(group):
-    return pl.BlockSpec((PLANE, GROUP, 8, ENC), lambda i, place: (0, group, 0, 0))
-
-
-WORK = [pltpu.VMEM((2 * HEAD_DIM, ENC), jnp.bfloat16), pltpu.VMEM((GROUP * HEAD_DIM, 2 * ROWS), jnp.bfloat16)]
+    return pl.BlockSpec((TOK, HEAD_DIM), lambda i, place: (0, head_of(i, place[0], place[1], offsets)))
+
+
+def part_of(group):
+    return jax.ShapeDtypeStruct((PLANE, group, 8, ENC), jnp.bfloat16)
+
+
+def work(group):
+    return [pltpu.VMEM((2 * HEAD_DIM, ENC), jnp.bfloat16), pltpu.VMEM((group * HEAD_DIM, 2 * ROWS), jnp.bfloat16)]
 
 
 def attend_near(place, own, other, tokens, weights, interpret=False):
     head = head_block(NEAR)
+    group = len(weights)
     return pl.pallas_call(
         near_body,
         grid_spec=pltpu.PrefetchScalarGridSpec(
             num_scalar_prefetch=1,
-            grid=(GROUP,),
-            in_specs=[whole(ROWS, EXT)] * 2 + [head] * 4 + [whole(2, HEAD_DIM, ENC)] * 4,
-            out_specs=[head, head, part_block(0), whole(2 * ROWS, ENC), whole(2 * ROWS, 128)],
-            scratch_shapes=WORK,
+            grid=(group,),
+            in_specs=[whole(ROWS, EXT)] * 2 + [head] * 4 + [whole(2, HEAD_DIM, ENC)] * group,
+            out_specs=[head, head, whole(PLANE, group, 8, ENC), whole(2 * ROWS, ENC), whole(2 * ROWS, 128)],
+            scratch_shapes=work(group),
         ),
         out_shape=[
             WIDE,
             WIDE,
-            PART,
+            part_of(group),
             jax.ShapeDtypeStruct((2 * ROWS, ENC), jnp.bfloat16),
             jax.ShapeDtypeStruct((2 * ROWS, 128), jnp.bfloat16),
         ],
@@ -190,73 +192,60 @@
     )(place, own, other, *tokens, *weights)
 
 
-def attend_far(place, rows, mask, tokens, weights, gq, gq2, part, interpret=False):
+def attend_far(place, rows, mask, tokens, weights, gq, gq2, interpret=False):
     head = head_block(FAR)
+    group = weights.shape[2]
     kv = lambda pick: pl.BlockSpec((PLANE, 1, 1, 8, ENC), lambda i, place: (0, pick(place[0]), i, 0, 0))
     kept = pl.BlockSpec(memory_space=pl.ANY)
     return pl.pallas_call(
         far_body,
         grid_spec=pltpu.PrefetchScalarGridSpec(
             num_scalar_prefetch=1,
-            grid=(GROUP,),
+            grid=(group,),
             in_specs=[whole(2 * ROWS, ENC), whole(2 * ROWS, 128)]
             + [head] * 4
             + [kv(lambda c: c), kv(lambda c: 1 - c)]
-            + [kept] * 3,
-            out_specs=[head, head, part_block(1)],
-            scratch_shapes=WORK,
+            + [kept] * 2,
+            out_specs=[head, head, whole(PLANE, group, 8, ENC)],
+            scratch_shapes=work(group),
         ),
-        out_shape=[WIDE, WIDE, PART],
-        input_output_aliases={9: 0, 10: 1, 11: 2},
+        out_shape=[WIDE, WIDE, part_of(group)],
+        input_output_aliases={9: 0, 10: 1},
         interpret=interpret,
         name="far",
-    )(place, rows, mask, *tokens, weights, weights, gq, gq2, part)
-
-
-def deal_body(place_ref, mine_ref, theirs_ref, kept_ref, given_ref):
-    kept_ref[...] = mine_ref[...]
-    given_ref[...] = theirs_ref[...]
+    )(place, rows, mask, *tokens, weights, weights, gq, gq2)
+
+
+def deal_body(place_ref, heads_ref, kept_ref, given_ref):
+    c, z = place_ref[0], place_ref[1]
+    for i in range(len(FAR[0])):
+        kept_ref[i] = heads_ref[head_of(i, c, z, FAR)]
+        given_ref[i] = heads_ref[head_of(i, 1 - c, z, FAR)]
+
+
+SMEM = pl.BlockSpec(memory_space=pltpu.SMEM)
+VMEM = pl.BlockSpec(memory_space=pltpu.VMEM)
 
 
 def deal(place, heads, interpret=False):
-    row = lambda index: pl.BlockSpec((1, 8, ENC), index)
-    out = row(lambda i, place: (i, 0, 0))
-    shape = jax.ShapeDtypeStruct((GROUP, 8, ENC), jnp.bfloat16)
-    return pl.pallas_call(
-        deal_body,
-        grid_spec=pltpu.PrefetchScalarGridSpec(
-            num_scalar_prefetch=1,
-            grid=(GROUP,),
-            in_specs=[
-                row(lambda i, place: (head_of(i, place, FAR), 0, 0)),
-                row(lambda i, place: (head_of(i, place, FAR[::-1]), 0, 0)),
-            ],
-            out_specs=[out, out],
-        ),
-        out_shape=[shape, shape],
-        interpret=interpret,
-        name="deal",
-    )(place, heads, heads)
-
-
-def gather_body(place_ref, part_ref, out_ref):
-    out_ref[...] = jnp.sum(part_ref[...].astype(jnp.float32), axis=0).astype(jnp.bfloat16)
-
-
-def gather(place, part, interpret=False):
-    both = tuple(n + f for n, f in zip(NEAR, FAR))
-    return pl.pallas_call(
-        gather_body,
-        grid_spec=pltpu.PrefetchScalarGridSpec(
-            num_scalar_prefetch=1,
-            grid=(HALF,),
-            in_specs=[pl.BlockSpec((PLANE, 1, 8, ENC), lambda i, place: (0, i, 0, 0))],
-            out_specs=pl.BlockSpec((1, 8, ENC), lambda i, place: (head_of(i, place, both), 0, 0)),
-        ),
-        out_shape=jax.ShapeDtypeStruct((HEADS, 8, ENC), jnp.bfloat16),
-        interpret=interpret,
-        name="gather",
-    )(place, part)
+    shape = jax.ShapeDtypeStruct((len(FAR[0]), 8, ENC), jnp.bfloat16)
+    return pl.pallas_call(
+        deal_body, out_shape=[shape, shape], in_specs=[SMEM, VMEM], out_specs=[VMEM] * 2, interpret=interpret, name="deal"
+    )(place, heads)
+
+
+def gather_body(place_ref, near_ref, far_ref, out_ref):
+    c, z = place_ref[0], place_ref[1]
+    for ref, offsets in ((near_ref, NEAR), (far_ref, FAR)):
+        for i in range(len(offsets[0])):
+            out_ref[head_of(i, c, z, offsets)] = jnp.sum(ref[:, i].astype(jnp.float32), axis=0).astype(jnp.bfloat16)
+
+
+def gather(place, near, far, interpret=False):
+    shape = jax.ShapeDtypeStruct((HEADS, 8, ENC), jnp.bfloat16)
+    return pl.pallas_call(
+        gather_body, out_shape=shape, in_specs=[SMEM, VMEM, VMEM], out_specs=VMEM, interpret=interpret, name="gather"
+    )(place, near, far)
 
 
 def swap(array):
@@ -275,14 +264,14 @@
     return array.astype(jnp.float32).sum(0)
 
 
-def fetch(array, even, odd):
+def fetch(array, turns):
     pairs = []
     for c in range(2):
         for z in range(HEADS):
-            turn = odd if (c + z) % 2 else even
-            core = 1 - c if (turn % 2 == 0) == (even != 0) else c
+            turn = turns[(c + z) % 2 * (1 + c)]
+            core = 1 - c if (turn % 2 == 0) == (turns[0] != 0) else c
             pairs.append((core * HEADS + (z + turn) % HEADS, c * HEADS + z))
-    assert len({a for a, _ in pairs}) == len(pairs)
+    assert len({source for source, _ in pairs}) == len(pairs)
     return lax.ppermute(array, ("c", "z"), pairs)
 
 
@@ -295,7 +284,9 @@
     heads = spread(piece, "z", HEADS)
     kept, given = deal(place, heads)
     mine = jnp.stack([kept, swap(given)])
-    near = [fetch(w_kv, even, odd) for even, odd in zip(*NEAR)]
+    near = []
+    for turns in zip(*NEAR):
+        near.append(fetch(w_kv, turns))
 
     packed = pack(counts, owner_rank, owner_span, encodings)
     arrived = exchange(packed.reshape(PLANE, 2 * CAP, EXT), ("y", "x")).reshape(ROWS, EXT)
@@ -304,9 +295,11 @@
     tokens = (queries, grad_ctx, swap(queries), swap(grad_ctx))
 
     gq, gq2, part, rows, mask = attend_near(place, arrived, other, tokens, near)
-    gq, gq2, part = attend_far(place, rows, mask, tokens, weights, gq, gq2, part)
-
-    sums = gather(place, exchange(part, ("y", "x")))
+    near_part = exchange(part, ("y", "x"))
+    gq, gq2, part = attend_far(place, rows, mask, tokens, weights, gq, gq2)
+    far_part = exchange(part, ("y", "x"))
+
+    sums = gather(place, near_part, far_part)
     final = (total(exchange(sums, "z")) / DP).astype(jnp.bfloat16)
     block = spread(final, ("y", "x"), PLANE).reshape(HEAD_DIM, ENC)
     grad_value = jnp.where(z % 2 == c, block, swap(block))

time: 240 us -> 209 us (0.87)
  waiting for transfers between devices: 66.6 us -> 43.3 us
  blocking collectives: 32.4 us -> 19.5 us
  starting transfers between devices: 81.3 us -> 93.6 us
  Pallas kernels: 42.8 us -> 37.3 us
    ppermute x4 -> x3, waiting for transfers between devices: 44.5 us -> 21.2 us  [fetch(): return lax.ppermute(array, ('c', 'z'), pairs)]
    all_to_all x1, blocking collectives: 32.4 us -> 19.5 us  [exchange(): return lax.all_to_all(array, axis, split_axis=0, concat_axis=0, tiled=True)]
    all_to_all x5 -> x6, starting transfers between devices: 36.6 us -> 48.8 us  [exchange(): return lax.all_to_all(array, axis, split_axis=0, concat_axis=0, tiled=True)]
    pallas_call x2, Pallas kernels: 9.46 us -> 4.16 us  [the longest x1 2.49 us: gather(): pl.pallas_call(gather_body, out_shape=shape, in_specs=[SMEM, VMEM, VMEM],...]
    pallas_call x1, Pallas kernels: 16.3 us -> 13.3 us  [attend_near(): pl.pallas_call(near_body, grid_spec=pltpu.PrefetchScalarGridSpec(num_scal...]
    pallas_call x1, Pallas kernels: 14.3 us -> 17.1 us  [attend_far(): pl.pallas_call(far_body, grid_spec=pltpu.PrefetchScalarGridSpec(num_scala...]
    ppermute x6, starting transfers between devices: 29.1 us -> 31.6 us  [swap(): return lax.ppermute(array, 'c', [(0, 1), (1, 0)])]
    ppermute x4 -> x3, starting transfers between devices: 15.5 us -> 13.2 us  [fetch(): return lax.ppermute(array, ('c', 'z'), pairs)]
  transfers between devices with their start and end apart: 15 -> 15, of which waited for: 7 -> 7; matrix products, arithmetic and copies ran while one was open for 3% -> 3% of each run, Pallas kernels for 9% -> 17%
where the time goes in v1:
time: 209 us; the launch traced here: 207 us
  starting transfers between devices  93.6 us (45%)
  waiting for transfers between devices  43.3 us (21%)
  Pallas kernels  37.3 us (18%)
  blocking collectives  19.5 us (9%)
  local copies, waits for them, and re-layouts  8.49 us (4%)
  other arithmetic  3.8 us (2%)
    all_to_all x6, starting transfers between devices, exchange(): return lax.all_to_all(array, axis, split_axis=0, concat_axis=0, tiled=True)  48.8 us
    ppermute x6, starting transfers between devices, swap(): return lax.ppermute(array, 'c', [(0, 1), (1, 0)])  31.6 us
    ppermute x3, waiting for transfers between devices, fetch(): return lax.ppermute(array, ('c', 'z'), pairs)  21.2 us
    all_to_all x6, waiting for transfers between devices, exchange(): return lax.all_to_all(array, axis, split_axis=0, concat_axis=0, tiled=True)  21 us
    all_to_all x1, blocking collectives, exchange(): return lax.all_to_all(array, axis, split_axis=0, concat_axis=0, tiled=True)  19.5 us
    pallas_call x1, Pallas kernels, attend_far(): pl.pallas_call(far_body, grid_spec=pltpu.PrefetchScalarGridSpec(num_scala...  17.1 us
    pallas_call x1, Pallas kernels, attend_near(): pl.pallas_call(near_body, grid_spec=pltpu.PrefetchScalarGridSpec(num_scal...  13.3 us
    ppermute x3, starting transfers between devices, fetch(): return lax.ppermute(array, ('c', 'z'), pairs)  13.2 us
  transfers between devices with their start and end apart: 15, of which 7 were waited for; matrix products, arithmetic and copies ran while one was open for 3% of the time, Pallas kernels for 17%

profile of v1, /device:TPU:1, one launch (start us, length us, event | category | flops | bytes accessed | tf_op | source)
XLA Modules:
  0.0 207.4 jit_solution(8883627531174229445)
XLA Ops:
  2.1 15.7 %all-to-all-start.1 = ((bf16[16,8,896]{2,1,0:T(8,128)(2,1)}), bf16[16,8,896]{2,1,0:T(8,128)(2,1)S(1)}, u32[]{:S(2)}, u32[]{:S(2)}) async-start(bf16[16,8,896]{2,1,0:T(8,128)(2,1)} %broadcast_in_dim.9), calls=%async_computation.1 | async-start | bytes 458752 | tf_op jit(solution)/shard_map/all_to_all | solution.py:256
  21.0 2.8 %pack.1 = bf16[384,1024]{1,0:T(8,128)(2,1)} custom-call(s32[1]{0:T(128)S(6)} %copy.13.count_ref, s32[1,384]{1,0:T(1,128)} %reshape.24.rank_ref, s32[1,384]{1,0:T(1,128)} %reshape.25.span_ref, bf16[384,896]{1,0:T(8,128)(2,1)} %enc_ref.1), custom_call_target="tpu_custom_call" | custom-call | tf_op jit(solution)/shard_map/pack/pallas_call | solution.py:50
  23.7 6.7 %all-to-all-done.1.heads_ref = bf16[16,8,896]{2,1,0:T(8,128)(2,1)S(1)} async-done(((bf16[16,8,896]{2,1,0:T(8,128)(2,1)}), bf16[16,8,896]{2,1,0:T(8,128)(2,1)S(1)}, u32[]{:S(2)}, u32[]{:S(2)}) %all-to-all-start.1) | async-done | bytes 229408 | tf_op jit(solution)/shard_map/all_to_all | solution.py:256
  30.5 6.8 %all-to-all-start = ((bf16[16,24,1024]{2,1,0:T(8,128)(2,1)}), bf16[16,24,1024]{2,1,0:T(8,128)(2,1)S(1)}, u32[]{:S(2)}, u32[]{:S(2)}) async-start(bf16[16,24,1024]{2,1,0:T(8,128)(2,1)} %bitcast.12), calls=%async_computation | async-start | bytes 1572864 | tf_op jit(solution)/shard_map/all_to_all | solution.py:256
  39.5 7.6 %collective-permute-start.6 = (bf16[5,8,896]{2,1,0:T(8,128)(2,1)}, bf16[5,8,896]{2,1,0:T(8,128)(2,1)S(1)}, u32[]{:S(2)}, u32[]{:S(2)}) collective-permute-start(bf16[5,8,896]{2,1,0:T(8,128)(2,1)} %get-tuple-element.15), channel_id=1, source_target_pairs={{0,16},{16,0},{1,17},{17,1},{2,18},{18,2},{3,19},{19,3},{4,20},{20... | collective-permute-start | bytes 215048 | tf_op jit(solution)/shard_map/ppermute | solution.py:252
  50.9 7.1 %all-to-all-start.2 = ((bf16[16,2,5,8,896]{4,3,2,1,0:T(8,128)(2,1)}), bf16[16,2,5,8,896]{4,3,2,1,0:T(8,128)(2,1)S(1)}, u32[]{:S(2)}, u32[]{:S(2)}) async-start(bf16[16,2,5,8,896]{4,3,2,1,0:T(8,128)(2,1)} %broadcast_in_dim.10), calls=%async_computation.2 | async-start | bytes 4587520 | tf_op jit(solution)/shard_map/all_to_all | solution.py:256
  57.9 4.1 %collective-permute-start.1 = (bf16[256,2048]{1,0:T(8,128)(2,1)S(1)}, bf16[256,2048]{1,0:T(8,128)(2,1)S(1)}, u32[]{:S(2)}, u32[]{:S(2)}) collective-permute-start(bf16[256,2048]{1,0:T(8,128)(2,1)S(1)} %copy-done.1), channel_id=1, source_target_pairs={{0,16},{16,0},{1,17},{17,1},{2,18},{18,2},{3,19},{19,3},{4,20},{20... | collective-permute-start | bytes 3145736 | tf_op jit(solution)/shard_map/ppermute | solution.py:252
  62.1 1.9 collective-permute-start.2
  64.0 6.3 %collective-permute-start.3 = (bf16[2,128,896]{2,1,0:T(8,128)(2,1)}, bf16[2,128,896]{2,1,0:T(8,128)(2,1)S(1)}, u32[]{:S(2)}, u32[]{:S(2)}) collective-permute-start(bf16[2,128,896]{2,1,0:T(8,128)(2,1)} %param.8), channel_id=1, source_target_pairs={{18,0},{2,1},{20,2},{4,3},{22,4},{6,5},{24,6},{8,7},{26,8},{10,9},... | collective-permute-start | bytes 1376264 | tf_op jit(solution)/shard_map/ppermute | solution.py:275
  72.2 3.1 %collective-permute-start.4 = (bf16[2,128,896]{2,1,0:T(8,128)(2,1)}, bf16[2,128,896]{2,1,0:T(8,128)(2,1)S(1)}, u32[]{:S(2)}, u32[]{:S(2)}) collective-permute-start(bf16[2,128,896]{2,1,0:T(8,128)(2,1)} %param.8), channel_id=1, source_target_pairs={{30,0},{0,1},{16,2},{2,3},{18,4},{4,5},{20,6},{6,7},{22,8},{8,9},{... | collective-permute-start | bytes 1376264 | tf_op jit(solution)/shard_map/ppermute | solution.py:275
  75.3 10.4 %collective-permute-done.3.w0_ref = bf16[2,128,896]{2,1,0:T(8,128)(2,1)S(1)} collective-permute-done((bf16[2,128,896]{2,1,0:T(8,128)(2,1)}, bf16[2,128,896]{2,1,0:T(8,128)(2,1)S(1)}, u32[]{:S(2)}, u32[]{:S(2)}) %collective-permute-start.3) | collective-permute-done | bytes 458784 | tf_op jit(solution)/shard_map/ppermute | solution.py:275
  85.7 3.9 %collective-permute-start.5 = (bf16[2,128,896]{2,1,0:T(8,128)(2,1)}, bf16[2,128,896]{2,1,0:T(8,128)(2,1)S(1)}, u32[]{:S(2)}, u32[]{:S(2)}) collective-permute-start(bf16[2,128,896]{2,1,0:T(8,128)(2,1)} %param.8), channel_id=1, source_target_pairs={{0,0},{20,1},{2,2},{22,3},{4,4},{24,5},{6,6},{26,7},{8,8},{28,9},{... | collective-permute-start | bytes 1376264 | tf_op jit(solution)/shard_map/ppermute | solution.py:275
  91.4 8.9 %collective-permute-done.5.w2_ref = bf16[2,128,896]{2,1,0:T(8,128)(2,1)S(1)} collective-permute-done((bf16[2,128,896]{2,1,0:T(8,128)(2,1)}, bf16[2,128,896]{2,1,0:T(8,128)(2,1)S(1)}, u32[]{:S(2)}, u32[]{:S(2)}) %collective-permute-start.5) | collective-permute-done | bytes 458784 | tf_op jit(solution)/shard_map/ppermute | solution.py:275
  102.5 13.3 %near.1 = (bf16[256,2048]{1,0:T(8,128)(2,1)}, bf16[256,2048]{1,0:T(8,128)(2,1)}, bf16[16,3,8,896]{3,2,1,0:T(8,128)(2,1)}, bf16[768,896]{1,0:T(8,128)(2,1)}, bf16[768,128]{1,0:T(8,128)(2,1)}) custom-call(s32[2]{0:T(128)} %pad_add_fusion.place_ref, bf16[384,1024]{1,0:T(8,128)(2,1)} %bitcast.11, bf16[384,1024]{1,0:T(8,128)(2,1)} %collective-permute-done.other_ref, ...), custom_call_target="tpu_custom_call" | custom-call | tf_op jit(solution)/shard_map/near/pallas_call | solution.py:174
  115.8 6.9 %all-to-all-start.3 = ((bf16[16,3,8,896]{3,2,1,0:T(8,128)(2,1)}), bf16[16,3,8,896]{3,2,1,0:T(8,128)(2,1)S(1)}, u32[]{:S(2)}, u32[]{:S(2)}) async-start(bf16[16,3,8,896]{3,2,1,0:T(8,128)(2,1)} %get-tuple-element.20), calls=%async_computation.3 | async-start | bytes 1376256 | tf_op jit(solution)/shard_map/all_to_all | solution.py:256
  122.7 17.1 %far.1 = (bf16[256,2048]{1,0:T(8,128)(2,1)}, bf16[256,2048]{1,0:T(8,128)(2,1)}, bf16[16,5,8,896]{3,2,1,0:T(8,128)(2,1)}) custom-call(s32[2]{0:T(128)} %pad_add_fusion.place_ref, bf16[768,896]{1,0:T(8,128)(2,1)} %get-tuple-element.12.rows_ref, bf16[768,128]{1,0:T(8,128)(2,1)} %get-tuple-element.13.mask_ref, ...), custom_call_target="tpu_custom_call", output_to_operand_aliasing={{0}: (9, {}), {1}: (10, {})} | custom-call | tf_op jit(solution)/shard_map/far/pallas_call | solution.py:200
  139.8 19.5 %all_to_all.35.far_ref = bf16[16,5,8,896]{3,2,1,0:T(8,128)(2,1)} all-to-all(bf16[16,5,8,896]{3,2,1,0:T(8,128)(2,1)} %get-tuple-element.21), channel_id=1, replica_groups=mesh['y'=4,'x'=4,'c'=2,'z'=16] {'y','x'}, dimensions={0} | all-to-all | bytes 2293760 | tf_op jit(solution)/shard_map/all_to_all | solution.py:256
  159.2 2.5 %gather.1 = bf16[16,8,896]{2,1,0:T(8,128)(2,1)} custom-call(s32[2]{0:T(128)} %pad_add_fusion.place_ref, bf16[16,3,8,896]{3,2,1,0:T(8,128)(2,1)} %copy-done.6, bf16[16,5,8,896]{3,2,1,0:T(8,128)(2,1)} %all_to_all.35.far_ref), custom_call_target="tpu_custom_call" | custom-call | tf_op jit(solution)/shard_map/gather/pallas_call | solution.py:246
  161.7 8.9 %all-to-all-start.5 = ((bf16[16,8,896]{2,1,0:T(8,128)(2,1)}), bf16[16,8,896]{2,1,0:T(8,128)(2,1)S(1)}, u32[]{:S(2)}, u32[]{:S(2)}) async-start(bf16[16,8,896]{2,1,0:T(8,128)(2,1)} %gather.1), calls=%async_computation.5 | async-start | bytes 458752 | tf_op jit(solution)/shard_map/all_to_all | solution.py:256
  170.6 5.6 %collective-permute-start.7 = (bf16[256,2048]{1,0:T(8,128)(2,1)}, bf16[256,2048]{1,0:T(8,128)(2,1)S(1)}, u32[]{:S(2)}, u32[]{:S(2)}) collective-permute-start(bf16[256,2048]{1,0:T(8,128)(2,1)} %get-tuple-element.19), channel_id=1, source_target_pairs={{0,16},{16,0},{1,17},{17,1},{2,18},{18,2},{3,19},{19,3},{4,20},{20... | collective-permute-start | bytes 3145736 | tf_op jit(solution)/shard_map/ppermute | solution.py:252
  176.2 6.9 %all-to-all-done.5 = bf16[16,8,896]{2,1,0:T(8,128)(2,1)S(1)} async-done(((bf16[16,8,896]{2,1,0:T(8,128)(2,1)}), bf16[16,8,896]{2,1,0:T(8,128)(2,1)S(1)}, u32[]{:S(2)}, u32[]{:S(2)}) %all-to-all-start.5) | async-done | bytes 229408 | tf_op jit(solution)/shard_map/all_to_all | solution.py:256
  183.9 3.5 %all-to-all-start.6 = ((bf16[16,8,896]{2,1,0:T(8,128)(2,1)}), bf16[16,8,896]{2,1,0:T(8,128)(2,1)S(1)}, u32[]{:S(2)}, u32[]{:S(2)}) async-start(bf16[16,8,896]{2,1,0:T(8,128)(2,1)} %broadcast_in_dim.22), calls=%async_computation.6 | async-start | bytes 458752 | tf_op jit(solution)/shard_map/all_to_all | solution.py:256
  187.4 7.3 %all-to-all-done.6 = bf16[16,8,896]{2,1,0:T(8,128)(2,1)S(1)} async-done(((bf16[16,8,896]{2,1,0:T(8,128)(2,1)}), bf16[16,8,896]{2,1,0:T(8,128)(2,1)S(1)}, u32[]{:S(2)}, u32[]{:S(2)}) %all-to-all-start.6) | async-done | bytes 229408 | tf_op jit(solution)/shard_map/all_to_all | solution.py:256
  194.7 10.4 %collective-permute-start.8 = (bf16[128,896]{1,0:T(8,128)(2,1)S(1)}, bf16[128,896]{1,0:T(8,128)(2,1)S(1)}, u32[]{:S(2)}, u32[]{:S(2)}) collective-permute-start(bf16[128,896]{1,0:T(8,128)(2,1)S(1)} %bitcast.13), channel_id=1, source_target_pairs={{0,16},{16,0},{1,17},{17,1},{2,18},{18,2},{3,19},{19,3},{4,20},{20... | collective-permute-start | bytes 688136 | tf_op jit(solution)/shard_map/ppermute | solution.py:252
  (48 shorter events, 18.8 us)
Async XLA Ops:
  2.1 28.4 %all-to-all-start.1 = ((bf16[16,8,896]{2,1,0:T(8,128)(2,1)}), bf16[16,8,896]{2,1,0:T(8,128)(2,1)S(1)}, u32[]{:S(2)}, u32[]{:S(2)}) async-start(bf16[16,8,896]{2,1,0:T(8,128)(2,1)} %broadcast_in_dim.9), calls=%async_computation.1 | async-start | bytes 458752 | tf_op jit(solution)/shard_map/all_to_all | solution.py:256
  30.5 7.3 %copy-start.7 = (bf16[16,8,896]{2,1,0:T(8,128)(2,1)}, bf16[16,8,896]{2,1,0:T(8,128)(2,1)S(1)}, u32[]{:S(2)}) copy-start(bf16[16,8,896]{2,1,0:T(8,128)(2,1)S(1)} %all-to-all-done.1.heads_ref) | copy-start | bytes 688132
  30.5 18.7 %all-to-all-start = ((bf16[16,24,1024]{2,1,0:T(8,128)(2,1)}), bf16[16,24,1024]{2,1,0:T(8,128)(2,1)S(1)}, u32[]{:S(2)}, u32[]{:S(2)}) async-start(bf16[16,24,1024]{2,1,0:T(8,128)(2,1)} %bitcast.12), calls=%async_computation | async-start | bytes 1572864 | tf_op jit(solution)/shard_map/all_to_all | solution.py:256
  39.5 8.7 %collective-permute-start.6 = (bf16[5,8,896]{2,1,0:T(8,128)(2,1)}, bf16[5,8,896]{2,1,0:T(8,128)(2,1)S(1)}, u32[]{:S(2)}, u32[]{:S(2)}) collective-permute-start(bf16[5,8,896]{2,1,0:T(8,128)(2,1)} %get-tuple-element.15), channel_id=1, source_target_pairs={{0,16},{16,0},{1,17},{17,1},{2,18},{18,2},{3,19},{19,3},{4,20},{20... | collective-permute-start | bytes 215048 | tf_op jit(solution)/shard_map/ppermute | solution.py:252
  49.1 1.7 copy-start.5
  50.8 7.1 %copy-start.1 = (bf16[256,2048]{1,0:T(8,128)(2,1)S(1)}, bf16[256,2048]{1,0:T(8,128)(2,1)}, u32[]{:S(2)}) copy-start(bf16[256,2048]{1,0:T(8,128)(2,1)} %q_ref.3) | copy-start | bytes 3145732
  50.9 64.9 %all-to-all-start.2 = ((bf16[16,2,5,8,896]{4,3,2,1,0:T(8,128)(2,1)}), bf16[16,2,5,8,896]{4,3,2,1,0:T(8,128)(2,1)S(1)}, u32[]{:S(2)}, u32[]{:S(2)}) async-start(bf16[16,2,5,8,896]{4,3,2,1,0:T(8,128)(2,1)} %broadcast_in_dim.10), calls=%async_computation.2 | async-start | bytes 4587520 | tf_op jit(solution)/shard_map/all_to_all | solution.py:256
  57.9 42.4 %collective-permute-start.1 = (bf16[256,2048]{1,0:T(8,128)(2,1)S(1)}, bf16[256,2048]{1,0:T(8,128)(2,1)S(1)}, u32[]{:S(2)}, u32[]{:S(2)}) collective-permute-start(bf16[256,2048]{1,0:T(8,128)(2,1)S(1)} %copy-done.1), channel_id=1, source_target_pairs={{0,16},{16,0},{1,17},{17,1},{2,18},{18,2},{3,19},{19,3},{4,20},{20... | collective-permute-start | bytes 3145736 | tf_op jit(solution)/shard_map/ppermute | solution.py:252
  62.1 39.3 %collective-permute-start.2 = (bf16[256,2048]{1,0:T(8,128)(2,1)}, bf16[256,2048]{1,0:T(8,128)(2,1)S(1)}, u32[]{:S(2)}, u32[]{:S(2)}) collective-permute-start(bf16[256,2048]{1,0:T(8,128)(2,1)} %g_ref.3), channel_id=1, source_target_pairs={{0,16},{16,0},{1,17},{17,1},{2,18},{18,2},{3,19},{19,3},{4,20},{20... | collective-permute-start | bytes 3145736 | tf_op jit(solution)/shard_map/ppermute | solution.py:252
  64.0 21.7 %collective-permute-start.3 = (bf16[2,128,896]{2,1,0:T(8,128)(2,1)}, bf16[2,128,896]{2,1,0:T(8,128)(2,1)S(1)}, u32[]{:S(2)}, u32[]{:S(2)}) collective-permute-start(bf16[2,128,896]{2,1,0:T(8,128)(2,1)} %param.8), channel_id=1, source_target_pairs={{18,0},{2,1},{20,2},{4,3},{22,4},{6,5},{24,6},{8,7},{26,8},{10,9},... | collective-permute-start | bytes 1376264 | tf_op jit(solution)/shard_map/ppermute | solution.py:275
  70.3 32.2 %collective-permute-start = (bf16[384,1024]{1,0:T(8,128)(2,1)}, bf16[384,1024]{1,0:T(8,128)(2,1)}, u32[]{:S(2)}, u32[]{:S(2)}) collective-permute-start(bf16[384,1024]{1,0:T(8,128)(2,1)} %bitcast.10), channel_id=1, source_target_pairs={{0,16},{16,0},{1,17},{17,1},{2,18},{18,2},{3,19},{19,3},{4,20},{20... | collective-permute-start | bytes 2359304 | tf_op jit(solution)/shard_map/ppermute | solution.py:252
  72.2 19.2 %collective-permute-start.4 = (bf16[2,128,896]{2,1,0:T(8,128)(2,1)}, bf16[2,128,896]{2,1,0:T(8,128)(2,1)S(1)}, u32[]{:S(2)}, u32[]{:S(2)}) collective-permute-start(bf16[2,128,896]{2,1,0:T(8,128)(2,1)} %param.8), channel_id=1, source_target_pairs={{30,0},{0,1},{16,2},{2,3},{18,4},{4,5},{20,6},{6,7},{22,8},{8,9},{... | collective-permute-start | bytes 1376264 | tf_op jit(solution)/shard_map/ppermute | solution.py:275
  85.7 15.6 %copy-start.8 = (bf16[2,128,896]{2,1,0:T(8,128)(2,1)}, bf16[2,128,896]{2,1,0:T(8,128)(2,1)S(1)}, u32[]{:S(2)}) copy-start(bf16[2,128,896]{2,1,0:T(8,128)(2,1)S(1)} %collective-permute-done.3.w0_ref) | copy-start | bytes 1376260
  85.7 14.6 %collective-permute-start.5 = (bf16[2,128,896]{2,1,0:T(8,128)(2,1)}, bf16[2,128,896]{2,1,0:T(8,128)(2,1)S(1)}, u32[]{:S(2)}, u32[]{:S(2)}) collective-permute-start(bf16[2,128,896]{2,1,0:T(8,128)(2,1)} %param.8), channel_id=1, source_target_pairs={{0,0},{20,1},{2,2},{22,3},{4,4},{24,5},{6,6},{26,7},{8,8},{28,9},{... | collective-permute-start | bytes 1376264 | tf_op jit(solution)/shard_map/ppermute | solution.py:275
  91.4 10.0 %copy-start.9 = (bf16[2,128,896]{2,1,0:T(8,128)(2,1)}, bf16[2,128,896]{2,1,0:T(8,128)(2,1)S(1)}, u32[]{:S(2)}) copy-start(bf16[2,128,896]{2,1,0:T(8,128)(2,1)S(1)} %collective-permute-done.4.w1_ref) | copy-start | bytes 1376260
  100.3 1.2 copy-start.10
  115.8 6.9 %copy-start = (bf16[16,2,5,8,896]{4,3,2,1,0:T(8,128)(2,1)}, bf16[16,2,5,8,896]{4,3,2,1,0:T(8,128)(2,1)S(1)}, u32[]{:S(2)}) copy-start(bf16[16,2,5,8,896]{4,3,2,1,0:T(8,128)(2,1)S(1)} %all-to-all-done.2.wk_ref.wv_ref) | copy-start | bytes 6881284
  115.8 24.0 %all-to-all-start.3 = ((bf16[16,3,8,896]{3,2,1,0:T(8,128)(2,1)}), bf16[16,3,8,896]{3,2,1,0:T(8,128)(2,1)S(1)}, u32[]{:S(2)}, u32[]{:S(2)}) async-start(bf16[16,3,8,896]{3,2,1,0:T(8,128)(2,1)} %get-tuple-element.20), calls=%async_computation.3 | async-start | bytes 1376256 | tf_op jit(solution)/shard_map/all_to_all | solution.py:256
  139.8 19.5 %copy-start.6 = (bf16[16,3,8,896]{3,2,1,0:T(8,128)(2,1)}, bf16[16,3,8,896]{3,2,1,0:T(8,128)(2,1)S(1)}, u32[]{:S(2)}) copy-start(bf16[16,3,8,896]{3,2,1,0:T(8,128)(2,1)S(1)} %all-to-all-done.3.near_ref) | copy-start | bytes 2064388
  159.2 45.9 %copy-start.4 = (bf16[256,2048]{1,0:T(8,128)(2,1)S(1)}, bf16[256,2048]{1,0:T(8,128)(2,1)}, u32[]{:S(2)}) copy-start(bf16[256,2048]{1,0:T(8,128)(2,1)} %get-tuple-element.18) | copy-start | bytes 3145732
  161.7 21.4 %all-to-all-start.5 = ((bf16[16,8,896]{2,1,0:T(8,128)(2,1)}), bf16[16,8,896]{2,1,0:T(8,128)(2,1)S(1)}, u32[]{:S(2)}, u32[]{:S(2)}) async-start(bf16[16,8,896]{2,1,0:T(8,128)(2,1)} %gather.1), calls=%async_computation.5 | async-start | bytes 458752 | tf_op jit(solution)/shard_map/all_to_all | solution.py:256
  170.6 34.6 %collective-permute-start.7 = (bf16[256,2048]{1,0:T(8,128)(2,1)}, bf16[256,2048]{1,0:T(8,128)(2,1)S(1)}, u32[]{:S(2)}, u32[]{:S(2)}) collective-permute-start(bf16[256,2048]{1,0:T(8,128)(2,1)} %get-tuple-element.19), channel_id=1, source_target_pairs={{0,16},{16,0},{1,17},{17,1},{2,18},{18,2},{3,19},{19,3},{4,20},{20... | collective-permute-start | bytes 3145736 | tf_op jit(solution)/shard_map/ppermute | solution.py:252
  183.9 10.9 %all-to-all-start.6 = ((bf16[16,8,896]{2,1,0:T(8,128)(2,1)}), bf16[16,8,896]{2,1,0:T(8,128)(2,1)S(1)}, u32[]{:S(2)}, u32[]{:S(2)}) async-start(bf16[16,8,896]{2,1,0:T(8,128)(2,1)} %broadcast_in_dim.22), calls=%async_computation.6 | async-start | bytes 458752 | tf_op jit(solution)/shard_map/all_to_all | solution.py:256
  194.7 12.0 %collective-permute-start.8 = (bf16[128,896]{1,0:T(8,128)(2,1)S(1)}, bf16[128,896]{1,0:T(8,128)(2,1)S(1)}, u32[]{:S(2)}, u32[]{:S(2)}) collective-permute-start(bf16[128,896]{1,0:T(8,128)(2,1)S(1)} %bitcast.13), channel_id=1, source_target_pairs={{0,16},{16,0},{1,17},{17,1},{2,18},{18,2},{3,19},{19,3},{4,20},{20... | collective-permute-start | bytes 688136 | tf_op jit(solution)/shard_map/ppermute | solution.py:252
  (2 other events, 2.0 us)
